TPU v7x, 32 devices: a whole 2x2x4 slice. The times are simulated.
32 devices in a mesh: slides: 2 (over y), rows: 8 (over z, x), cols: 2 (over core).
Axes of the slice: x: 2, y: 2, z: 4, core: 2. Of those that a mesh axis runs over, the one named last changes fastest.
Arguments:
- tokens: bfloat16 [512, 32, 512], P(('slides', 'cols'), 'rows'), parts along dimension 0, may hold values from -6 to 6
- norm_gain: float32 [512], replicated, may hold values from 0.5 to 1.5
- w_in: bfloat16 [512, 2048], replicated, may hold values from -0.25 to 0.25
- w_bc: bfloat16 [512, 64], replicated, may hold values from -0.046875 to 0.046875
- rate_row: float32 [16, 1024], replicated, may hold values from 0.002 to 0.08
- rate_col: float32 [16, 1024], replicated, may hold values from 0.002 to 0.08
- skip_gain: float32 [1024], replicated, may hold values from 0.5 to 1.5
- w_out: bfloat16 [1024, 512], replicated, may hold values from -0.1875 to 0.1875
Outputs:
- mixed: bfloat16 [512, 32, 512], P(('slides', 'cols'), 'rows'), parts along dimension 0
There are 2 independent parts, one for each index of `slides`. A program takes and returns all parts, laid end to end along the dimension named above; an argument that names none is the same for every part. Nothing has to cross between parts.
All inputs are finite; a program needn't handle non-finite values.
Results may differ from a plain program's by a relative error of at most 0.013.
Values may be sent and summed in bfloat16 or wider, within the bound.
A program may use at most 64 MiB of HBM per device.

v0:
```python
import jax
import jax.numpy as jnp
from jax import lax
from jax.sharding import PartitionSpec as P


def prefix(shard, axis, combine, identity):
    size, here = (lax.axis_size(axis), lax.axis_index(axis))
    everything = jax.tree.map(
        lambda part, kind: lax.all_gather(part.astype(kind), axis),
        shard,
        (jnp.bfloat16, jnp.bfloat16),
    )
    start = jax.tree.map(
        lambda part, zero: jnp.broadcast_to(jnp.asarray(zero, part.dtype), part.shape),
        shard,
        identity,
    )

    def turn(k, before):
        reached = k < here
        new = combine(
            before, jax.tree.map(lambda part, own: part[k].astype(own.dtype), everything, shard)
        )
        return jax.tree.map(lambda a, b: jnp.where(reached, a, b), new, before)

    return lax.fori_loop(0, size, turn, start)


def block_scan(series, inject, readout, decay_factor, skip_weight, scan_axis):
    block_len = 16
    other_axis = 1 - scan_axis
    item_count = series.shape[other_axis]
    start_state = jnp.zeros((item_count, decay_factor.shape[0], decay_factor.shape[1]), jnp.float32)
    start_out = jnp.zeros(series.shape, jnp.float32)

    def one_block(block_id, carry):
        carried, outputs = carry
        first_row = block_id * block_len
        series_part = lax.dynamic_slice_in_dim(series, first_row, block_len, scan_axis).astype(
            jnp.float32
        )
        inject_part = lax.dynamic_slice_in_dim(inject, first_row, block_len, scan_axis).astype(
            jnp.float32
        )
        readout_part = lax.dynamic_slice_in_dim(readout, first_row, block_len, scan_axis).astype(
            jnp.float32
        )
        results = []
        for offset in range(block_len):
            value_now = lax.index_in_dim(series_part, offset, scan_axis, keepdims=False)
            inject_now = lax.index_in_dim(inject_part, offset, scan_axis, keepdims=False)
            read_now = lax.index_in_dim(readout_part, offset, scan_axis, keepdims=False)
            carried = decay_factor[None] * carried + inject_now[:, :, None] * value_now[:, None, :]
            results.append(
                jnp.einsum("ine,in->ie", carried, read_now, precision=lax.Precision.HIGHEST)
                + skip_weight * value_now
            )
        stacked = jnp.stack(results, axis=scan_axis)
        outputs = lax.dynamic_update_slice_in_dim(outputs, stacked, first_row, scan_axis)
        return (carried, outputs)

    carried, outputs = lax.fori_loop(
        0, series.shape[scan_axis] // block_len, one_block, (start_state, start_out)
    )
    return (outputs, carried)


def chain_join(earlier, later):
    return (earlier[0] * later[0], later[0][None] * earlier[1] + later[1])


def per_device(tokens, norm_gain, w_in, w_bc, rate_row, rate_col, skip_gain, w_out):
    inner_width = w_out.shape[0]
    state_width = rate_row.shape[0]
    as_float = tokens.astype(jnp.float32)
    scale_now = lax.rsqrt(jnp.mean(as_float * as_float, axis=-1, keepdims=True) + 1e-05)
    normed = (as_float * scale_now * norm_gain).astype(jnp.bfloat16)
    project = jnp.dot(normed, w_in, preferred_element_type=jnp.float32)
    inputs_u = project[..., :inner_width].astype(jnp.bfloat16)
    gate_z = project[..., inner_width:].astype(jnp.bfloat16)
    mixers = jnp.dot(normed, w_bc, preferred_element_type=jnp.float32).astype(jnp.bfloat16)
    col_vectors = mixers[..., 2 * state_width :]
    moved_u, moved_vectors = (
        lax.all_to_all(inputs_u, "rows", split_axis=0, concat_axis=1, tiled=True),
        lax.all_to_all(
            mixers[..., : 2 * state_width], "rows", split_axis=0, concat_axis=1, tiled=True
        ),
    )
    row_out, _ = block_scan(
        moved_u,
        moved_vectors[..., :state_width],
        moved_vectors[..., state_width:],
        jnp.exp(-rate_row),
        skip_gain,
        1,
    )
    row_mixed = row_out.astype(jnp.bfloat16)
    back_home = lax.all_to_all(row_mixed, "rows", split_axis=1, concat_axis=0, tiled=True)
    col_readout = col_vectors[..., state_width:]
    col_out, end_state = block_scan(
        back_home, col_vectors[..., :state_width], col_readout, jnp.exp(-rate_col), 1.0, 0
    )
    height = back_home.shape[0]
    total_decay = jnp.exp(-rate_col * height)
    incoming = prefix(
        (total_decay, end_state),
        "cols",
        chain_join,
        (jnp.ones_like(total_decay), jnp.zeros_like(end_state)),
    )[1]

    def correct(block_id, outputs):
        first_row = block_id * 16
        read_part = lax.dynamic_slice_in_dim(col_readout, first_row, 16, 0).astype(jnp.float32)
        steps_ahead = (first_row + 1 + jnp.arange(16, dtype=jnp.int32)).astype(jnp.float32)
        powers = jnp.exp(-rate_col[None] * steps_ahead[:, None, None])
        carried_part = jnp.einsum(
            "lwn,lne,wne->lwe", read_part, powers, incoming, precision=lax.Precision.HIGHEST
        )
        updated = lax.dynamic_slice_in_dim(outputs, first_row, 16, 0) + carried_part
        return lax.dynamic_update_slice_in_dim(outputs, updated, first_row, 0)

    col_out = lax.fori_loop(0, height // 16, correct, col_out)
    gated = (col_out * jax.nn.silu(gate_z.astype(jnp.float32))).astype(jnp.bfloat16)
    return jnp.dot(gated, w_out, preferred_element_type=jnp.float32).astype(jnp.bfloat16)


def solution(mesh):
    placed = (P(("slides", "cols"), "rows", None), P(), P(), P(), P(), P(), P(), P())
    return jax.shard_map(
        per_device,
        mesh=mesh,
        in_specs=placed,
        out_specs=P(("slides", "cols"), "rows", None),
        check_vma=False,
    )
```

profile of v0, /device:TPU:0, one launch (start us, length us, event | category | flops | bytes accessed | tf_op | source)
XLA Modules:
  0.0 232.9 jit_solution(4700963122558836914)
XLA Ops:
  0.0 1.5 fusion.184
  1.6 1.4 fusion.186
  5.0 7.3 %all-to-all-start = ((bf16[8,2,1024]{2,1,0:T(2,128)(2,1)}), bf16[8,2,1024]{2,1,0:T(2,128)(2,1)S(1)}, u32[]{:S(2)}, u32[]{:S(2)}) async-start(bf16[8,2,1024]{2,1,0:T(2,128)(2,1)} %reshape.149), calls=%async_computation | async-start | bytes 65536 | tf_op jit(solution)/shard_map/all_to_all | solution.py:86
  12.3 1.3 convolution_convert_fusion
  13.6 1.3 copy-done.5
  15.1 1.8 copy.78
  16.9 2.1 all-to-all-done
  19.0 3.8 %all-to-all-start.1 = ((bf16[128,4,1024]{2,1,0:T(4,128)(2,1)}), bf16[128,4,1024]{2,1,0:T(4,128)(2,1)S(1)}, u32[]{:S(2)}, u32[]{:S(2)}) async-start(bf16[128,4,1024]{2,1,0:T(4,128)(2,1)} %copy.78), calls=%async_computation.1 | async-start | bytes 2097152 | tf_op jit(solution)/shard_map/all_to_all | solution.py:85
  23.9 24.4 %all-to-all-done.1 = bf16[128,4,1024]{2,1,0:T(4,128)(2,1)S(1)} async-done(((bf16[128,4,1024]{2,1,0:T(4,128)(2,1)}), bf16[128,4,1024]{2,1,0:T(4,128)(2,1)S(1)}, u32[]{:S(2)}, u32[]{:S(2)}) %all-to-all-start.1) | async-done | bytes 1048608 | tf_op jit(solution)/shard_map/all_to_all | solution.py:85
  48.3 1.3 copy.79
  50.7 44.3 %while.62 = (s32[]{:T(128)}, f32[16,16,1024]{2,1,0:T(8,128)}, bf16[16,32,1024]{2,0,1:T(8,128)(2,1)}, f32[16,1024]{1,0:T(8,128)S(1)}, bf16[16,32,16]{2,0,1:T(8,12...) while((s32[]{:T(128)}, f32[16,16,1024]{2,1,0:T(8,128)}, ...), condition=%wide.region_2.0_spmd.clone, body=%wide.region_1.0_spmd.clone.sunk | while | flops 94638096 | bytes 42889080 | solution.py:63
  50.7 1.5 fusion.296
  52.2 1.2 dynamic-slice_convert_fusion.6
  54.1 1.4 fusion.297
  55.5 1.5 fusion.298
  60.3 1.3 fusion.302
  61.7 2.3 multiply_add_fusion.115
  72.3 1.5 fusion.296
  75.6 2.0 fusion.297
  77.7 2.0 fusion.298
  83.0 1.3 fusion.302
  84.4 2.3 multiply_add_fusion.115
  95.1 4.4 %all-to-all-start.2 = ((bf16[16,32,1024]{2,0,1:T(8,128)(2,1)}), bf16[16,32,1024]{2,0,1:T(8,128)(2,1)}, u32[]{:S(2)}, u32[]{:S(2)}) async-start(bf16[16,32,1024]{2,0,1:T(8,128)(2,1)} %get-tuple-element.491), calls=%async_computation.2 | async-start | bytes 2097152 | tf_op jit(solution)/shard_map/all_to_all | solution.py:99
  99.7 1.9 all-gather
  101.5 23.3 %all-to-all-done.2 = bf16[16,32,1024]{2,0,1:T(8,128)(2,1)} async-done(((bf16[16,32,1024]{2,0,1:T(8,128)(2,1)}), bf16[16,32,1024]{2,0,1:T(8,128)(2,1)}, u32[]{:S(2)}, u32[]{:S(2)}) %all-to-all-start.2) | async-done | bytes 1048608 | tf_op jit(solution)/shard_map/all_to_all | solution.py:99
  124.8 3.0 %copy.80 = bf16[16,8,4,1024]{3,2,0,1:T(4,128)(2,1)} copy(bf16[16,8,4,1024]{3,0,2,1:T(8,128)(2,1)} %bitcast.13) | data formatting | bytes 2097152 | tf_op jit(solution)/shard_map/all_to_all | solution.py:99
  127.9 1.8 broadcast_in_dim.18
  129.7 69.7 %while.63 = (s32[]{:T(128)}, f32[4,16,1024]{2,1,0:T(8,128)S(1)}, f32[128,4,1024]{2,1,0:T(4,128)}, f32[16,1024]{1,0:T(8,128)S(1)}, bf16[128,4,16]{0,2,1:T(8,128)(...) while((s32[]{:T(128)}, f32[4,16,1024]{2,1,0:T(8,128)S(1)}, ...), condition=%wide.region_4.0_spmd.clone, body=%wide.region_3.0_spmd.clone.sunk | while | flops 27526164 | bytes 9698083 | solution.py:63
  199.5 2.0 all-gather.1
  201.8 26.2 %while.61 = (s32[]{:T(128)}, f32[128,4,1024]{2,1,0:T(4,128)}, f32[1,16,1024]{2,1,0:T(8,128)S(1)}, bf16[128,4,16]{2,1,0:T(4,128)(2,1)S(1)}, f32[4,16,1024]{2,1,0:...) while((s32[]{:T(128)}, f32[128,4,1024]{2,1,0:T(4,128)}, f32[1,16,1024]{2,1,0:T(8,128)S(1)}, ...), condition=%wide.region_8.9_spmd, body=%wide.region_7.8_spmd.sunk | while | flops 3408935 | bytes 3483939 | solution.py:124
  202.1 1.3 multiply_reduce_fusion.2
  203.4 1.7 fusion.275
  205.4 1.3 multiply_reduce_fusion.2
  206.7 1.8 fusion.275
  208.6 1.3 multiply_reduce_fusion.2
  210.0 1.7 fusion.275
  211.9 1.3 multiply_reduce_fusion.2
  213.2 1.7 fusion.275
  215.2 1.3 multiply_reduce_fusion.2
  216.5 1.8 fusion.275
  218.5 1.3 multiply_reduce_fusion.2
  219.8 1.7 fusion.275
  221.7 1.3 multiply_reduce_fusion.2
  223.0 1.7 fusion.275
  225.0 1.3 multiply_reduce_fusion.2
  226.3 1.7 fusion.275
  228.0 3.7 %convolution_convert_fusion.1 = bf16[128,4,512]{2,0,1:T(8,128)(2,1)S(1)} fusion(bf16[1024,512]{1,0:T(8,128)(2,1)} %param.23, f32[128,4,1024]{2,1,0:T(4,128)} %get-tuple-element.495, bf16[128,4,2048]{2,0,1:T(8,128)(2,1)} %copy-done.5), kind=kOutput, calls=%fused_computation.390 | convolution fusion | flops 540803072 | bytes 4718592 | tf_op jit(solution)/shard_map/dot_general | solution.py:126
  231.7 1.2 copy.85
  (504 shorter events, 99.9 us)
Async XLA Ops:
  0.0 12.3 %copy-start = (bf16[512,2048]{1,0:T(8,128)(2,1)S(1)}, bf16[512,2048]{1,0:T(8,128)(2,1)}, u32[]{:S(2)}) copy-start(bf16[512,2048]{1,0:T(8,128)(2,1)} %param.18) | copy-start | bytes 6291460
  4.1 0.9 copy-start.17
  5.0 14.0 %all-to-all-start = ((bf16[8,2,1024]{2,1,0:T(2,128)(2,1)}), bf16[8,2,1024]{2,1,0:T(2,128)(2,1)S(1)}, u32[]{:S(2)}, u32[]{:S(2)}) async-start(bf16[8,2,1024]{2,1,0:T(2,128)(2,1)} %reshape.149), calls=%async_computation | async-start | bytes 65536 | tf_op jit(solution)/shard_map/all_to_all | solution.py:86
  13.6 1.4 copy-start.5
  15.1 7.8 %copy-start.16 = (f32[16,1024]{1,0:T(8,128)S(1)}, f32[16,1024]{1,0:T(8,128)}, u32[]{:S(2)}) copy-start(f32[16,1024]{1,0:T(8,128)} %param.20) | copy-start | bytes 196612
  19.0 29.3 %all-to-all-start.1 = ((bf16[128,4,1024]{2,1,0:T(4,128)(2,1)}), bf16[128,4,1024]{2,1,0:T(4,128)(2,1)S(1)}, u32[]{:S(2)}, u32[]{:S(2)}) async-start(bf16[128,4,1024]{2,1,0:T(4,128)(2,1)} %copy.78), calls=%async_computation.1 | async-start | bytes 2097152 | tf_op jit(solution)/shard_map/all_to_all | solution.py:85
  23.0 27.7 %copy-start.3 = (f32[1024]{0:T(1024)S(1)}, f32[1024]{0:T(1024)}, u32[]{:S(2)}) copy-start(f32[1024]{0:T(1024)} %param.22) | copy-start | bytes 12292
  54.1 3.0 %copy-start.1 = (f32[16,16,1024]{2,1,0:T(8,128)S(1)}, f32[16,16,1024]{2,1,0:T(8,128)}, u32[]{:S(2)}) copy-start(f32[16,16,1024]{2,1,0:T(8,128)} %get-tuple-element.1202) | copy-start | bytes 3145732 | tf_op jit(solution)/shard_map/while
  54.1 3.0 %copy-start.4 = (f32[16,16]{1,0:T(8,128)S(1)}, f32[16,16]{1,0:T(8,128)}, u32[]{:S(2)}) copy-start(f32[16,16]{1,0:T(8,128)} %get-tuple-element.1055) | copy-start | bytes 3076 | tf_op jit(solution)/shard_map/while
  54.1 3.0 %copy-start.14 = (bf16[16,16,1]{1,0,2:T(8,128)(2,1)S(1)}, bf16[16,16,1]{1,0,2:T(8,128)(2,1)}, u32[]{:S(2)}) copy-start(bf16[16,16,1]{1,0,2:T(8,128)(2,1)} %get-tuple-element.1058) | copy-start | bytes 1540 | tf_op jit(solution)/shard_map/while
  57.0 1.0 copy-start.13
  58.0 1.1 copy-start.12
  59.1 1.2 copy-start.11
  61.7 2.3 copy-start.10
  64.0 7.0 %copy-start.2 = (f32[16,16,1024]{2,1,0:T(8,128)}, f32[16,16,1024]{2,1,0:T(8,128)S(1)}, u32[]{:S(2)}) copy-start(f32[16,16,1024]{2,1,0:T(8,128)S(1)} %get-tuple-element.1229) | copy-start | bytes 3145732 | tf_op jit(solution)/shard_map/while
  64.0 1.0 copy-start.9
  65.0 0.9 copy-start.8
  65.9 1.5 copy-start.7
  66.7 1.6 copy-start.6
  75.6 4.1 %copy-start.1 = (f32[16,16,1024]{2,1,0:T(8,128)S(1)}, f32[16,16,1024]{2,1,0:T(8,128)}, u32[]{:S(2)}) copy-start(f32[16,16,1024]{2,1,0:T(8,128)} %get-tuple-element.1202) | copy-start | bytes 3145732 | tf_op jit(solution)/shard_map/while
  75.6 4.1 %copy-start.4 = (f32[16,16]{1,0:T(8,128)S(1)}, f32[16,16]{1,0:T(8,128)}, u32[]{:S(2)}) copy-start(f32[16,16]{1,0:T(8,128)} %get-tuple-element.1055) | copy-start | bytes 3076 | tf_op jit(solution)/shard_map/while
  75.6 4.1 %copy-start.14 = (bf16[16,16,1]{1,0,2:T(8,128)(2,1)S(1)}, bf16[16,16,1]{1,0,2:T(8,128)(2,1)}, u32[]{:S(2)}) copy-start(bf16[16,16,1]{1,0,2:T(8,128)(2,1)} %get-tuple-element.1058) | copy-start | bytes 1540 | tf_op jit(solution)/shard_map/while
  79.7 1.0 copy-start.13
  80.7 1.1 copy-start.12
  81.8 1.2 copy-start.11
  84.3 2.3 copy-start.10
  86.7 7.0 %copy-start.2 = (f32[16,16,1024]{2,1,0:T(8,128)}, f32[16,16,1024]{2,1,0:T(8,128)S(1)}, u32[]{:S(2)}) copy-start(f32[16,16,1024]{2,1,0:T(8,128)S(1)} %get-tuple-element.1229) | copy-start | bytes 3145732 | tf_op jit(solution)/shard_map/while
  86.7 1.0 copy-start.9
  87.7 0.9 copy-start.8
  88.6 1.5 copy-start.7
  89.4 1.6 copy-start.6
  95.0 4.4 %copy-start.18 = (bf16[128,4,64]{0,2,1:T(8,128)(2,1)S(1)}, bf16[128,4,64]{0,2,1:T(8,128)(2,1)}, u32[]{:S(2)}) copy-start(bf16[128,4,64]{0,2,1:T(8,128)(2,1)} %copy-done.17) | copy-start | bytes 196612
  95.0 4.6 %copy-start.15 = (f32[16,1024]{1,0:T(8,128)S(1)}, f32[16,1024]{1,0:T(8,128)}, u32[]{:S(2)}) copy-start(f32[16,1024]{1,0:T(8,128)} %param.21) | copy-start | bytes 196612
  95.1 29.8 %all-to-all-start.2 = ((bf16[16,32,1024]{2,0,1:T(8,128)(2,1)}), bf16[16,32,1024]{2,0,1:T(8,128)(2,1)}, u32[]{:S(2)}, u32[]{:S(2)}) async-start(bf16[16,32,1024]{2,0,1:T(8,128)(2,1)} %get-tuple-element.491), calls=%async_computation.2 | async-start | bytes 2097152 | tf_op jit(solution)/shard_map/all_to_all | solution.py:99
where the time goes:
time: 234 us; the launch traced here: 233 us
  matrix products  81.9 us (35%)
  other arithmetic  51.2 us (22%)
  waiting for transfers between devices  49.9 us (21%)
  local copies, waits for them, and re-layouts  27.4 us (12%)
  starting transfers between devices  15.5 us (7%)
  blocking collectives  3.85 us (2%)
  loops' own time  3.01 us (1%)
    dot_general x160, matrix products, one_block(): jnp.einsum('ine,in->ie', carried, read_now, precision=lax.Precision.HIGHEST)  75.8 us
    all_to_all x1, waiting for transfers between devices, per_device(): lax.all_to_all(inputs_u, 'rows', split_axis=0, concat_axis=1, tiled=True)  24.4 us
    all_to_all x1, waiting for transfers between devices, per_device(): lax.all_to_all(row_mixed, 'rows', split_axis=1, concat_axis=0, tiled=True)  23.3 us
    dynamic_update_slice x8, other arithmetic, correct(): return lax.dynamic_update_slice_in_dim(outputs, updated, first_row, 0)  13.9 us
    dot_general x8, other arithmetic, correct(): jnp.einsum('lwn,lne,wne->lwe', read_part, powers, incoming, precision=lax...  10.4 us
    convert_element_type x10, other arithmetic, one_block(): lax.dynamic_slice_in_dim(series, first_row, block_len, scan_axis)  9.74 us
    add x10, other arithmetic, one_block(): decay_factor[None] * carried  9.09 us
    dynamic_update_slice x10, local copies, waits for them, and re-layouts, one_block(): lax.dynamic_update_slice_in_dim(outputs, stacked, first_row, scan_axis)  7.58 us
  transfers between devices with their start and end apart: 3, of which 3 were waited for; matrix products, arithmetic and copies ran while one was open for 2% of the time, Pallas kernels for 0%

commit v1 on v0

--- a/solution.py
+++ b/solution.py
@@ -2,6 +2,20 @@
 import jax.numpy as jnp
 from jax import lax
 from jax.sharding import PartitionSpec as P
+
+
+def tell_block(base_x, dim_i, inner_x):
+    carry_out, q_next = (base_x.shape[:dim_i], base_x.shape[dim_i + 1 :])
+    right_arr = base_x.reshape(*carry_out, inner_x, -1, *q_next)
+    local_next = jnp.moveaxis(right_arr, dim_i, 0)
+    return local_next
+
+
+def find_lane(arr, at_axis):
+    block_next = list(arr.shape[1:])
+    block_next[at_axis] *= arr.shape[0]
+    far_arr = jnp.moveaxis(arr, 0, at_axis).reshape(block_next)
+    return far_arr
 
 
 def prefix(shard, axis, combine, identity):
@@ -81,8 +95,24 @@
     gate_z = project[..., inner_width:].astype(jnp.bfloat16)
     mixers = jnp.dot(normed, w_bc, preferred_element_type=jnp.float32).astype(jnp.bfloat16)
     col_vectors = mixers[..., 2 * state_width :]
+
+    def _link_edge(body, along_axis, raw, local_x):
+        y1 = lax.axis_size(along_axis)
+        step_out = lax.axis_index(along_axis)
+        long_array, inter = (y1, step_out)
+        mixed_arr = tell_block(body, raw, long_array)
+        by_rank = [mixed_arr[inter]]
+        for i in [*range(1, long_array)]:
+            g_now = mixed_arr[inter ^ i]
+            out_arr = lax.ppermute(g_now, along_axis, [(j0, j0 ^ i) for j0 in range(long_array)])
+            by_rank.append(out_arr)
+        val2 = jnp.stack(by_rank)
+        mixed_arr = val2[inter ^ jnp.arange(long_array)]
+        state_next = find_lane(mixed_arr, local_x)
+        return state_next
+
     moved_u, moved_vectors = (
-        lax.all_to_all(inputs_u, "rows", split_axis=0, concat_axis=1, tiled=True),
+        _link_edge(inputs_u, "rows", 0, 1),
         lax.all_to_all(
             mixers[..., : 2 * state_width], "rows", split_axis=0, concat_axis=1, tiled=True
         ),

time: 234 us -> 226 us (0.966)
  waiting for transfers between devices: 49.9 us -> 30.1 us
  starting transfers between devices: 15.5 us -> 22.8 us
  local copies, waits for them, and re-layouts: 27.4 us -> 32 us
    all_to_all x1 -> x0, waiting for transfers between devices: 24.4 us -> none  [per_device(): lax.all_to_all(inputs_u, 'rows', split_axis=0, concat_axis=1, tiled=True)]
    ppermute x0 -> x7, starting transfers between devices: none -> 12.6 us  [_link_edge(): lax.ppermute(g_now, along_axis, [(j0, j0 ^ i) for j0 in range(long_array)])]
    unnamed x17 -> x29, local copies, waits for them, and re-layouts: 2.43 us -> 7.61 us
    all_to_all x1 -> x0, starting transfers between devices: 3.85 us -> none  [per_device(): lax.all_to_all(inputs_u, 'rows', split_axis=0, concat_axis=1, tiled=True)]
    all_to_all x1, waiting for transfers between devices: 2.15 us -> 5.79 us  [per_device(): lax.all_to_all(mixers[..., :2 * state_width], 'rows', split_axis=0, conca...]
    all_to_all x1, starting transfers between devices: 7.28 us -> 4.87 us  [per_device(): lax.all_to_all(mixers[..., :2 * state_width], 'rows', split_axis=0, conca...]
  transfers between devices with their start and end apart: 3 -> 9, of which waited for: 3 -> 3; matrix products, arithmetic and copies ran while one was open for 2% -> 3% of each run, Pallas kernels for 0% -> 0%
where the time goes in v1:
time: 226 us; the launch traced here: 225 us
  matrix products  81 us (36%)
  other arithmetic  52 us (23%)
  local copies, waits for them, and re-layouts  32 us (14%)
  waiting for transfers between devices  30.1 us (13%)
  starting transfers between devices  22.8 us (10%)
  blocking collectives  3.85 us (2%)
  loops' own time  3 us (1%)
    dot_general x160, matrix products, one_block(): jnp.einsum('ine,in->ie', carried, read_now, precision=lax.Precision.HIGHEST)  75.8 us
    all_to_all x1, waiting for transfers between devices, per_device(): lax.all_to_all(row_mixed, 'rows', split_axis=1, concat_axis=0, tiled=True)  22.2 us
    dynamic_update_slice x8, other arithmetic, correct(): return lax.dynamic_update_slice_in_dim(outputs, updated, first_row, 0)  13.8 us
    ppermute x7, starting transfers between devices, _link_edge(): lax.ppermute(g_now, along_axis, [(j0, j0 ^ i) for j0 in range(long_array)])  12.6 us
    dot_general x8, other arithmetic, correct(): jnp.einsum('lwn,lne,wne->lwe', read_part, powers, incoming, precision=lax...  10.4 us
    convert_element_type x10, other arithmetic, one_block(): lax.dynamic_slice_in_dim(series, first_row, block_len, scan_axis)  9.72 us
    add x10, other arithmetic, one_block(): decay_factor[None] * carried  9.09 us
    unnamed x29, local copies, waits for them, and re-layouts  7.61 us
  transfers between devices with their start and end apart: 9, of which 3 were waited for; matrix products, arithmetic and copies ran while one was open for 3% of the time, Pallas kernels for 0%

profile of v1, /device:TPU:0, one launch (start us, length us, event | category | flops | bytes accessed | tf_op | source)
XLA Modules:
  0.0 225.0 jit_solution(10001159427903383349)
XLA Ops:
  0.0 1.5 fusion.184
  1.6 1.4 fusion.186
  4.3 1.3 copy-done.6
  6.7 3.0 %collective-permute-start = (bf16[16,4,1024]{2,0,1:T(8,128)(2,1)}, bf16[16,4,1024]{2,0,1:T(8,128)(2,1)}, u32[]{:S(2)}, u32[]{:S(2)}) collective-permute-start(bf16[16,4,1024]{2,0,1:T(8,128)(2,1)} %get-tuple-element.797), channel_id=1, source_target_pairs={{0,2},{2,0},{4,6},{6,4},{8,10},{10,8},{12,14},{14,12},{1,3},{3,1},... | collective-permute-start | bytes 393224 | tf_op jit(solution)/shard_map/ppermute | solution.py:107
  9.7 1.6 collective-permute-start.1
  11.3 3.0 %collective-permute-start.3 = (bf16[16,4,1024]{2,0,1:T(8,128)(2,1)}, bf16[16,4,1024]{2,0,1:T(8,128)(2,1)}, u32[]{:S(2)}, u32[]{:S(2)}) collective-permute-start(bf16[16,4,1024]{2,0,1:T(8,128)(2,1)} %get-tuple-element.794), channel_id=1, source_target_pairs={{0,8},{2,10},{4,12},{6,14},{8,0},{10,2},{12,4},{14,6},{1,9},{3,11}... | collective-permute-start | bytes 393224 | tf_op jit(solution)/shard_map/ppermute | solution.py:107
  14.3 1.3 collective-permute-start.4
  17.4 4.9 %all-to-all-start = ((bf16[8,2,1024]{2,1,0:T(2,128)(2,1)}), bf16[8,2,1024]{2,1,0:T(2,128)(2,1)S(1)}, u32[]{:S(2)}, u32[]{:S(2)}) async-start(bf16[8,2,1024]{2,1,0:T(2,128)(2,1)} %reshape.181), calls=%async_computation | async-start | bytes 65536 | tf_op jit(solution)/shard_map/all_to_all | solution.py:116
  23.2 5.8 %all-to-all-done = bf16[8,2,1024]{2,1,0:T(2,128)(2,1)S(1)} async-done(((bf16[8,2,1024]{2,1,0:T(2,128)(2,1)}), bf16[8,2,1024]{2,1,0:T(2,128)(2,1)S(1)}, u32[]{:S(2)}, u32[]{:S(2)}) %all-to-all-start) | async-done | bytes 32800 | tf_op jit(solution)/shard_map/all_to_all | solution.py:116
  29.9 1.8 collective-permute-start.5
  32.7 2.0 collective-permute-start.6
  38.4 2.1 collective-permute-done.6
  40.5 1.6 gather_fusion
  43.2 44.3 %while.62 = (s32[]{:T(128)}, f32[16,16,1024]{2,1,0:T(8,128)}, bf16[16,32,1024]{2,0,1:T(8,128)(2,1)}, f32[16,1024]{1,0:T(8,128)S(1)}, bf16[16,32,16]{2,0,1:T(8,12...) while((s32[]{:T(128)}, f32[16,16,1024]{2,1,0:T(8,128)}, ...), condition=%wide.region_2.0_spmd.clone, body=%wide.region_1.0_spmd.clone.sunk | while | flops 94638096 | bytes 42889080 | solution.py:77
  43.2 1.5 fusion.297
  46.5 1.4 fusion.298
  48.0 1.5 fusion.299
  52.8 1.3 fusion.303
  54.2 2.3 %multiply_add_fusion.115 = (f32[16,16,1024]{2,1,0:T(8,128)S(1)}, f32[16,16,1024]{2,1,0:T(8,128)S(1)}, f32[16,16,1024]{2,1,0:T(8,128)S(1)}) fusion(f32[16,1024]{1,0:T(8,128)S(1)} %get-tuple-element.1081, f32[16,16]{1,0:T(8,128)S(1)} %get-tuple-element.1082, f32[16,1024]{1,0:T(8,128)S(1)} %get-tuple-element.1083, f32[16,16]{1,0:T(8,128)S(1)} %get-tuple-element.1084, ...), kind=kLoop, calls=%fused_computation.3.clone.1 | loop fusion | flops 12845056 | bytes 5324801 | tf_op jit(solution)/shard_map/while/body/eval_jaxpr/add | solution.py:68
  64.8 1.5 fusion.297
  68.1 2.0 fusion.298
  70.2 2.0 fusion.299
  76.9 2.3 %multiply_add_fusion.115 = (f32[16,16,1024]{2,1,0:T(8,128)S(1)}, f32[16,16,1024]{2,1,0:T(8,128)S(1)}, f32[16,16,1024]{2,1,0:T(8,128)S(1)}) fusion(f32[16,1024]{1,0:T(8,128)S(1)} %get-tuple-element.1081, f32[16,16]{1,0:T(8,128)S(1)} %get-tuple-element.1082, f32[16,1024]{1,0:T(8,128)S(1)} %get-tuple-element.1083, f32[16,16]{1,0:T(8,128)S(1)} %get-tuple-element.1084, ...), kind=kLoop, calls=%fused_computation.3.clone.1 | loop fusion | flops 12845056 | bytes 5324801 | tf_op jit(solution)/shard_map/while/body/eval_jaxpr/add | solution.py:68
  87.5 5.3 %all-to-all-start.1 = ((bf16[16,32,1024]{2,0,1:T(8,128)(2,1)}), bf16[16,32,1024]{2,0,1:T(8,128)(2,1)}, u32[]{:S(2)}, u32[]{:S(2)}) async-start(bf16[16,32,1024]{2,0,1:T(8,128)(2,1)} %get-tuple-element.491), calls=%async_computation.1 | async-start | bytes 2097152 | tf_op jit(solution)/shard_map/all_to_all | solution.py:129
  93.0 1.9 all-gather
  94.9 22.2 %all-to-all-done.1 = bf16[16,32,1024]{2,0,1:T(8,128)(2,1)} async-done(((bf16[16,32,1024]{2,0,1:T(8,128)(2,1)}), bf16[16,32,1024]{2,0,1:T(8,128)(2,1)}, u32[]{:S(2)}, u32[]{:S(2)}) %all-to-all-start.1) | async-done | bytes 1048608 | tf_op jit(solution)/shard_map/all_to_all | solution.py:129
  117.1 3.0 %copy.70 = bf16[16,8,4,1024]{3,2,0,1:T(4,128)(2,1)} copy(bf16[16,8,4,1024]{3,0,2,1:T(8,128)(2,1)} %bitcast.28) | data formatting | bytes 2097152 | tf_op jit(solution)/shard_map/all_to_all | solution.py:129
  120.1 1.9 broadcast_in_dim.18
  122.0 69.7 %while.63 = (s32[]{:T(128)}, f32[4,16,1024]{2,1,0:T(8,128)S(1)}, f32[128,4,1024]{2,1,0:T(4,128)}, f32[16,1024]{1,0:T(8,128)S(1)}, bf16[128,4,16]{0,2,1:T(8,128)(...) while((s32[]{:T(128)}, f32[4,16,1024]{2,1,0:T(8,128)S(1)}, ...), condition=%wide.region_4.0_spmd.clone, body=%wide.region_3.0_spmd.clone.sunk | while | flops 27526164 | bytes 9698083 | solution.py:77
  191.7 2.0 all-gather.1
  194.0 26.1 %while.61 = (s32[]{:T(128)}, f32[128,4,1024]{2,1,0:T(4,128)}, f32[1,16,1024]{2,1,0:T(8,128)S(1)}, bf16[128,4,16]{2,1,0:T(4,128)(2,1)S(1)}, f32[4,16,1024]{2,1,0:...) while((s32[]{:T(128)}, f32[128,4,1024]{2,1,0:T(4,128)}, f32[1,16,1024]{2,1,0:T(8,128)S(1)}, ...), condition=%wide.region_8.9_spmd, body=%wide.region_7.8_spmd.sunk | while | flops 3408935 | bytes 3483939 | solution.py:154
  194.3 1.3 multiply_reduce_fusion.2
  195.6 1.7 fusion.276
  197.5 1.3 multiply_reduce_fusion.2
  198.8 1.7 fusion.276
  200.8 1.3 multiply_reduce_fusion.2
  202.1 1.7 fusion.276
  204.0 1.3 multiply_reduce_fusion.2
  205.3 1.7 fusion.276
  207.3 1.3 multiply_reduce_fusion.2
  208.6 1.7 fusion.276
  210.6 1.3 multiply_reduce_fusion.2
  211.9 1.7 fusion.276
  213.8 1.3 multiply_reduce_fusion.2
  215.1 1.7 fusion.276
  217.1 1.3 multiply_reduce_fusion.2
  218.4 1.7 fusion.276
  220.1 3.7 %convolution_convert_fusion.1 = bf16[128,4,512]{2,0,1:T(8,128)(2,1)S(1)} fusion(bf16[1024,512]{1,0:T(8,128)(2,1)} %param.23, f32[128,4,1024]{2,1,0:T(4,128)} %get-tuple-element.495, bf16[128,4,2048]{2,0,1:T(8,128)(2,1)} %copy-done.6), kind=kOutput, calls=%fused_computation.391 | convolution fusion | flops 540803072 | bytes 4718592 | tf_op jit(solution)/shard_map/dot_general | solution.py:156
  (531 shorter events, 110.9 us)
Async XLA Ops:
  0.0 3.0 %copy-start = (bf16[512,2048]{1,0:T(8,128)(2,1)S(1)}, bf16[512,2048]{1,0:T(8,128)(2,1)}, u32[]{:S(2)}) copy-start(bf16[512,2048]{1,0:T(8,128)(2,1)} %param.18) | copy-start | bytes 6291460
  3.0 1.3 copy-start.7
  4.3 1.3 copy-start.6
  5.6 9.9 %copy-start.21 = (bf16[512,64]{0,1:T(8,128)(2,1)S(1)}, bf16[512,64]{0,1:T(8,128)(2,1)}, u32[]{:S(2)}) copy-start(bf16[512,64]{0,1:T(8,128)(2,1)} %param.19) | copy-start | bytes 196612
  5.7 9.8 %copy-start.8 = (bf16[128,4,512]{2,1,0:T(4,128)(2,1)S(1)}, bf16[128,4,512]{2,1,0:T(4,128)(2,1)}, u32[]{:S(2)}) copy-start(bf16[128,4,512]{2,1,0:T(4,128)(2,1)} %copy-done.7) | copy-start | bytes 1572868
  6.7 25.0 %copy-start.4 = (bf16[8,16,4,1024]{3,1,0,2:T(8,128)(2,1)S(1)}, bf16[8,16,4,1024]{3,1,0,2:T(8,128)(2,1)}, u32[]{:S(2)}) copy-start(bf16[8,16,4,1024]{3,1,0,2:T(8,128)(2,1)} %get-tuple-element.798) | copy-start | bytes 3145732
  6.7 23.2 %collective-permute-start = (bf16[16,4,1024]{2,0,1:T(8,128)(2,1)}, bf16[16,4,1024]{2,0,1:T(8,128)(2,1)}, u32[]{:S(2)}, u32[]{:S(2)}) collective-permute-start(bf16[16,4,1024]{2,0,1:T(8,128)(2,1)} %get-tuple-element.797), channel_id=1, source_target_pairs={{0,2},{2,0},{4,6},{6,4},{8,10},{10,8},{12,14},{14,12},{1,3},{3,1},... | collective-permute-start | bytes 393224 | tf_op jit(solution)/shard_map/ppermute | solution.py:107
  9.7 23.0 %collective-permute-start.1 = (bf16[16,4,1024]{2,0,1:T(8,128)(2,1)}, bf16[16,4,1024]{2,0,1:T(8,128)(2,1)}, u32[]{:S(2)}, u32[]{:S(2)}) collective-permute-start(bf16[16,4,1024]{2,0,1:T(8,128)(2,1)} %get-tuple-element.796), channel_id=1, source_target_pairs={{0,4},{2,6},{4,0},{6,2},{8,12},{10,14},{12,8},{14,10},{1,5},{3,7},... | collective-permute-start | bytes 393224 | tf_op jit(solution)/shard_map/ppermute | solution.py:107
  11.3 24.3 %collective-permute-start.2 = (bf16[16,4,1024]{2,0,1:T(8,128)(2,1)}, bf16[16,4,1024]{2,0,1:T(8,128)(2,1)}, u32[]{:S(2)}, u32[]{:S(2)}) collective-permute-start(bf16[16,4,1024]{2,0,1:T(8,128)(2,1)} %get-tuple-element.795), channel_id=1, source_target_pairs={{0,6},{2,4},{4,2},{6,0},{8,14},{10,12},{12,10},{14,8},{1,7},{3,5},... | collective-permute-start | bytes 393224 | tf_op jit(solution)/shard_map/ppermute | solution.py:107
  11.3 25.2 %collective-permute-start.3 = (bf16[16,4,1024]{2,0,1:T(8,128)(2,1)}, bf16[16,4,1024]{2,0,1:T(8,128)(2,1)}, u32[]{:S(2)}, u32[]{:S(2)}) collective-permute-start(bf16[16,4,1024]{2,0,1:T(8,128)(2,1)} %get-tuple-element.794), channel_id=1, source_target_pairs={{0,8},{2,10},{4,12},{6,14},{8,0},{10,2},{12,4},{14,6},{1,9},{3,11}... | collective-permute-start | bytes 393224 | tf_op jit(solution)/shard_map/ppermute | solution.py:107
  14.3 23.2 %collective-permute-start.4 = (bf16[16,4,1024]{2,0,1:T(8,128)(2,1)}, bf16[16,4,1024]{2,0,1:T(8,128)(2,1)}, u32[]{:S(2)}, u32[]{:S(2)}) collective-permute-start(bf16[16,4,1024]{2,0,1:T(8,128)(2,1)} %get-tuple-element.793), channel_id=1, source_target_pairs={{0,10},{2,8},{4,14},{6,12},{8,2},{10,0},{12,6},{14,4},{1,11},{3,9}... | collective-permute-start | bytes 393224 | tf_op jit(solution)/shard_map/ppermute | solution.py:107
  15.8 0.6 copy-start.19
  17.4 11.6 %all-to-all-start = ((bf16[8,2,1024]{2,1,0:T(2,128)(2,1)}), bf16[8,2,1024]{2,1,0:T(2,128)(2,1)S(1)}, u32[]{:S(2)}, u32[]{:S(2)}) async-start(bf16[8,2,1024]{2,1,0:T(2,128)(2,1)} %reshape.181), calls=%async_computation | async-start | bytes 65536 | tf_op jit(solution)/shard_map/all_to_all | solution.py:116
  29.9 8.4 %collective-permute-start.5 = (bf16[16,4,1024]{2,0,1:T(8,128)(2,1)}, bf16[16,4,1024]{2,0,1:T(8,128)(2,1)S(1)}, u32[]{:S(2)}, u32[]{:S(2)}) collective-permute-start(bf16[16,4,1024]{2,0,1:T(8,128)(2,1)} %get-tuple-element.792), channel_id=1, source_target_pairs={{0,12},{2,14},{4,8},{6,10},{8,4},{10,6},{12,0},{14,2},{1,13},{3,15... | collective-permute-start | bytes 393224 | tf_op jit(solution)/shard_map/ppermute | solution.py:107
  32.7 7.8 %collective-permute-start.6 = (bf16[16,4,1024]{2,0,1:T(8,128)(2,1)S(1)}, bf16[16,4,1024]{2,0,1:T(8,128)(2,1)S(1)}, u32[]{:S(2)}, u32[]{:S(2)}) collective-permute-start(bf16[16,4,1024]{2,0,1:T(8,128)(2,1)S(1)} %get-tuple-element.791), channel_id=1, source_target_pairs={{0,14},{2,12},{4,10},{6,8},{8,6},{10,4},{12,2},{14,0},{1,15},{3,13... | collective-permute-start | bytes 393224 | tf_op jit(solution)/shard_map/ppermute | solution.py:107
  36.5 6.7 %copy-start.3 = (f32[1024]{0:T(1024)S(1)}, f32[1024]{0:T(1024)}, u32[]{:S(2)}) copy-start(f32[1024]{0:T(1024)} %param.22) | copy-start | bytes 12292
  46.5 3.0 %copy-start.1 = (f32[16,16,1024]{2,1,0:T(8,128)S(1)}, f32[16,16,1024]{2,1,0:T(8,128)}, u32[]{:S(2)}) copy-start(f32[16,16,1024]{2,1,0:T(8,128)} %get-tuple-element.1210) | copy-start | bytes 3145732 | tf_op jit(solution)/shard_map/while
  46.5 3.0 %copy-start.5 = (f32[16,16]{1,0:T(8,128)S(1)}, f32[16,16]{1,0:T(8,128)}, u32[]{:S(2)}) copy-start(f32[16,16]{1,0:T(8,128)} %get-tuple-element.1063) | copy-start | bytes 3076 | tf_op jit(solution)/shard_map/while
  46.5 3.0 %copy-start.17 = (bf16[16,16,1]{1,0,2:T(8,128)(2,1)S(1)}, bf16[16,16,1]{1,0,2:T(8,128)(2,1)}, u32[]{:S(2)}) copy-start(bf16[16,16,1]{1,0,2:T(8,128)(2,1)} %get-tuple-element.1066) | copy-start | bytes 1540 | tf_op jit(solution)/shard_map/while
  49.5 1.0 copy-start.16
  50.5 1.1 copy-start.15
  51.6 1.2 copy-start.14
  54.2 2.3 %copy-start.13 = (bf16[16,16,1]{1,0,2:T(8,128)(2,1)S(1)}, bf16[16,16,1]{1,0,2:T(8,128)(2,1)}, u32[]{:S(2)}) copy-start(bf16[16,16,1]{1,0,2:T(8,128)(2,1)} %get-tuple-element.1113) | copy-start | bytes 1540 | tf_op jit(solution)/shard_map/while
  56.5 7.0 %copy-start.2 = (f32[16,16,1024]{2,1,0:T(8,128)}, f32[16,16,1024]{2,1,0:T(8,128)S(1)}, u32[]{:S(2)}) copy-start(f32[16,16,1024]{2,1,0:T(8,128)S(1)} %get-tuple-element.1237) | copy-start | bytes 3145732 | tf_op jit(solution)/shard_map/while
  56.5 1.0 copy-start.12
  57.5 0.9 copy-start.11
  58.4 1.5 copy-start.10
  59.2 1.6 copy-start.9
  68.1 4.1 %copy-start.1 = (f32[16,16,1024]{2,1,0:T(8,128)S(1)}, f32[16,16,1024]{2,1,0:T(8,128)}, u32[]{:S(2)}) copy-start(f32[16,16,1024]{2,1,0:T(8,128)} %get-tuple-element.1210) | copy-start | bytes 3145732 | tf_op jit(solution)/shard_map/while
  68.1 4.1 %copy-start.5 = (f32[16,16]{1,0:T(8,128)S(1)}, f32[16,16]{1,0:T(8,128)}, u32[]{:S(2)}) copy-start(f32[16,16]{1,0:T(8,128)} %get-tuple-element.1063) | copy-start | bytes 3076 | tf_op jit(solution)/shard_map/while
  68.1 4.1 %copy-start.17 = (bf16[16,16,1]{1,0,2:T(8,128)(2,1)S(1)}, bf16[16,16,1]{1,0,2:T(8,128)(2,1)}, u32[]{:S(2)}) copy-start(bf16[16,16,1]{1,0,2:T(8,128)(2,1)} %get-tuple-element.1066) | copy-start | bytes 1540 | tf_op jit(solution)/shard_map/while
  72.2 1.0 copy-start.16
  73.2 1.1 copy-start.15
  74.3 1.2 copy-start.14
  76.9 2.3 %copy-start.13 = (bf16[16,16,1]{1,0,2:T(8,128)(2,1)S(1)}, bf16[16,16,1]{1,0,2:T(8,128)(2,1)}, u32[]{:S(2)}) copy-start(bf16[16,16,1]{1,0,2:T(8,128)(2,1)} %get-tuple-element.1113) | copy-start | bytes 1540 | tf_op jit(solution)/shard_map/while
  79.2 7.0 %copy-start.2 = (f32[16,16,1024]{2,1,0:T(8,128)}, f32[16,16,1024]{2,1,0:T(8,128)S(1)}, u32[]{:S(2)}) copy-start(f32[16,16,1024]{2,1,0:T(8,128)S(1)} %get-tuple-element.1237) | copy-start | bytes 3145732 | tf_op jit(solution)/shard_map/while
  79.2 1.0 copy-start.12
  80.2 0.9 copy-start.11
  81.1 1.5 copy-start.10
  81.9 1.6 copy-start.9
  87.5 5.3 %copy-start.20 = (bf16[128,4,64]{0,2,1:T(8,128)(2,1)S(1)}, bf16[128,4,64]{0,2,1:T(8,128)(2,1)}, u32[]{:S(2)}) copy-start(bf16[128,4,64]{0,2,1:T(8,128)(2,1)} %copy-done.19) | copy-start | bytes 196612
  87.5 5.5 %copy-start.18 = (f32[16,1024]{1,0:T(8,128)S(1)}, f32[16,1024]{1,0:T(8,128)}, u32[]{:S(2)}) copy-start(f32[16,1024]{1,0:T(8,128)} %param.21) | copy-start | bytes 196612
  87.5 29.5 %all-to-all-start.1 = ((bf16[16,32,1024]{2,0,1:T(8,128)(2,1)}), bf16[16,32,1024]{2,0,1:T(8,128)(2,1)}, u32[]{:S(2)}, u32[]{:S(2)}) async-start(bf16[16,32,1024]{2,0,1:T(8,128)(2,1)} %get-tuple-element.491), calls=%async_computation.1 | async-start | bytes 2097152 | tf_op jit(solution)/shard_map/all_to_all | solution.py:129
